TPU v7x, 32 devices: a whole 2x2x4 slice. The times are simulated.
32 devices in a mesh: gy: 16 (over z, y, core), gz: 2 (over x).
Axes of the slice: x: 2, y: 2, z: 4, core: 2. Of those that a mesh axis runs over, the one named last changes fastest.
Arguments:
- initial_block: bfloat16 [16, 2, 2, 512, 512], P('gy', 'gz'), may hold values from -6 to 6
- tile_ops: bfloat16 [16, 2, 2, 512, 512], P('gy', 'gz'), may hold values from -0.125 to 0.125
- couple_ops: bfloat16 [16, 2, 4, 2, 512, 512], P('gy', 'gz'), may hold values from -0.125 to 0.125
- couple_map: int32 [16, 2, 4, 2], P('gy', 'gz'), may hold values from 0 to 1
- cell_scale: float32 [16, 2, 2, 512], P('gy', 'gz'), may hold values from 0.4 to 2.5
Outputs:
- basis: float32 [16, 2, 2, 512, 512], P('gy', 'gz')
- factor: float32 [512, 512], replicated
All inputs are finite; a program needn't handle non-finite values.
Results may differ from a plain program's by a relative error of at most 0.0053.
Values may be sent and summed in bfloat16 or wider, within the bound.
A program may use at most 64 MiB of HBM per device.

v0:
```python
import jax
import jax.numpy as jnp
from jax import lax
from jax.sharding import PartitionSpec as P


def shifted(block, axis, distance):
    devices = range(lax.axis_size(axis))
    route = [((i - distance) % len(devices), i) for i in devices]
    return lax.ppermute(block, axis, route)


def pick_tiles(blocks, indices):
    return jnp.take(blocks, indices, axis=0)


def neighbour_faces(scaled):
    y_from_lower = shifted(scaled, "gy", 1)
    y_from_upper = shifted(scaled, "gy", -1)
    z_from_lower = shifted(scaled, "gz", 1)
    z_from_upper = shifted(scaled, "gz", -1)
    faces = [y_from_lower[0, 0], y_from_upper[0, 0], z_from_lower[0, 0], z_from_upper[0, 0]]
    return jnp.stack(faces)


def apply_scaled(field, tile_ops, couple_ops, couple_map, cell_scale):
    scale_wide = cell_scale[..., None]
    scaled = (scale_wide * field).astype(jnp.bfloat16)
    inner = jnp.einsum(
        "tij,tjk->tik", tile_ops[0, 0], scaled[0, 0], preferred_element_type=jnp.float32
    )
    stacked = neighbour_faces(scaled)
    picked = jax.vmap(pick_tiles)(stacked, couple_map[0, 0])
    outer = jnp.einsum(
        "dtij,dtjk->tik", couple_ops[0, 0], picked, preferred_element_type=jnp.float32
    )
    return scale_wide * (inner + outer)[None, None]


def body(initial_block, tile_ops, couple_ops, couple_map, cell_scale):

    def filter_map(field):
        return (
            (1.0 - 1.1) * field - apply_scaled(field, tile_ops, couple_ops, couple_map, cell_scale)
        ) / 0.9

    first = initial_block.astype(jnp.float32)
    second = filter_map(first)
    third = 2.0 * filter_map(second) - first
    fourth = 2.0 * filter_map(third) - second
    width = fourth.shape[-1]
    flat = fourth.reshape(-1, width)
    total_cells = flat.shape[0] * lax.axis_size("gy") * lax.axis_size("gz")
    local_gram = jnp.einsum("ck,cl->kl", flat, flat, precision=lax.Precision.HIGHEST)
    gram = lax.psum(local_gram, ("gy", "gz"))
    gram = gram / jnp.float32(total_cells)
    lower = jnp.linalg.cholesky(gram)
    basis = jax.scipy.linalg.solve_triangular(lower, flat.T, lower=True).T
    return (basis.reshape(fourth.shape), lower.T)


def solution(mesh):
    placed = (
        P("gy", "gz", None, None, None),
        P("gy", "gz", None, None, None),
        P("gy", "gz", None, None, None, None),
        P("gy", "gz", None, None),
        P("gy", "gz", None, None),
    )
    return jax.shard_map(
        body,
        mesh=mesh,
        in_specs=placed,
        out_specs=(P("gy", "gz", None, None, None), P()),
        check_vma=False,
    )
```

profile of v0, /device:TPU:0, one launch (start us, length us, event | category | flops | bytes accessed | tf_op | source)
XLA Modules:
  0.0 432.5 jit_solution(8653095912852456125)
XLA Ops:
  9.4 5.0 %collective-permute-start.1 = (bf16[1,1,2,512,512]{4,3,2,1,0:T(8,128)(2,1)S(1)}, bf16[1,1,2,512,512]{4,3,2,1,0:T(8,128)(2,1)}, u32[]{:S(2)}, u32[]{:S(2)}) collective-permute-start(bf16[1,1,2,512,512]{4,3,2,1,0:T(8,128)(2,1)S(1)} %fusion.10), channel_id=1, source_target_pairs={{2,0},{4,2},{6,4},{8,6},{10,8},{12,10},{14,12},{16,14},{18,16},{20... | collective-permute-start | bytes 3145736 | tf_op jit(solution)/shard_map/ppermute | solution.py:10
  18.6 8.4 %collective-permute-done = bf16[1,1,2,512,512]{4,3,2,1,0:T(8,128)(2,1)S(1)} collective-permute-done((bf16[1,1,2,512,512]{4,3,2,1,0:T(8,128)(2,1)S(1)}, bf16[1,1,2,512,512]{4,3,2,1,0:T(8,128)(2,1)S(1)}, u32[]{:S(2)}, u32[]{:S(2)}) %collective-permute-start) | collective-permute-done | bytes 1048608 | tf_op jit(solution)/shard_map/ppermute | solution.py:10
  27.0 10.2 %collective-permute-done.2 = bf16[1,1,2,512,512]{4,3,2,1,0:T(8,128)(2,1)} collective-permute-done((bf16[1,1,2,512,512]{4,3,2,1,0:T(8,128)(2,1)S(1)}, bf16[1,1,2,512,512]{4,3,2,1,0:T(8,128)(2,1)}, u32[]{:S(2)}, u32[]{:S(2)}) %collective-permute-start.2) | collective-permute-done | bytes 1048608 | tf_op jit(solution)/shard_map/ppermute | solution.py:10
  37.2 3.9 pad_maximum_fusion
  41.1 5.1 %gather_fusion = bf16[8,512,512]{2,1,0:T(8,128)(2,1)} fusion(bf16[4,2,512,512]{3,2,1,0:T(8,128)(2,1)} %pad_maximum_fusion, s32[8]{0:T(128)S(1)} %reshape.120), kind=kCustom, calls=%fused_computation.clone | custom fusion | bytes 8388672 | tf_op jit(solution)/shard_map/vmap(jit(_take))/gather | solution.py:14
  46.2 7.5 %multiply_convert_fusion.1 = (bf16[1,1,2,512,512]{4,3,2,1,0:T(8,128)(2,1)S(1)}, f32[1,1,2,512,512]{4,3,2,1,0:T(8,128)}) fusion(f32[2,512]{1,0:T(2,128)S(1)} %broadcast_multiply_fusion.1, f32[2,512,512]{1,2,0:T(8,128)S(1)} %copy-done.4, bf16[4,2,512,512]{3,2,1,0:T(8,128)(2,1)} %bitcast.157, pred[4,2]{0,1:T(4,128)(4,1)S(1)} %compare_and_fusion, ...), kind=kOutput, calls=%fused_computation.43 | convolution fusion | flops 2153250816 | bytes 14688264 | tf_op jit(solution)/shard_map/dtij,dtjk->tik/dot_general | solution.py:34
  54.2 4.0 collective-permute-start.4
  60.4 10.4 %collective-permute-done.3 = bf16[1,1,2,512,512]{4,3,2,1,0:T(8,128)(2,1)S(1)} collective-permute-done((bf16[1,1,2,512,512]{4,3,2,1,0:T(8,128)(2,1)S(1)}, bf16[1,1,2,512,512]{4,3,2,1,0:T(8,128)(2,1)S(1)}, u32[]{:S(2)}, u32[]{:S(2)}) %collective-permute-start.3) | collective-permute-done | bytes 1048608 | tf_op jit(solution)/shard_map/ppermute | solution.py:10
  70.8 9.7 %collective-permute-done.5 = bf16[1,1,2,512,512]{4,3,2,1,0:T(8,128)(2,1)S(1)} collective-permute-done((bf16[1,1,2,512,512]{4,3,2,1,0:T(8,128)(2,1)S(1)}, bf16[1,1,2,512,512]{4,3,2,1,0:T(8,128)(2,1)S(1)}, u32[]{:S(2)}, u32[]{:S(2)}) %collective-permute-start.5) | collective-permute-done | bytes 1048608 | tf_op jit(solution)/shard_map/ppermute | solution.py:10
  80.5 2.3 pad_maximum_fusion.1
  82.7 4.9 %gather_fusion.1 = bf16[8,512,512]{2,1,0:T(8,128)(2,1)} fusion(bf16[4,2,512,512]{3,2,1,0:T(8,128)(2,1)} %pad_maximum_fusion.1, s32[8]{0:T(128)S(1)} %reshape.120), kind=kCustom, calls=%fused_computation.1.clone | custom fusion | bytes 8388672 | tf_op jit(solution)/shard_map/vmap(jit(_take))/gather | solution.py:14
  87.7 8.4 %multiply_convert_fusion = (bf16[1,1,2,512,512]{4,3,2,1,0:T(8,128)(2,1)S(1)}, f32[1,1,2,512,512]{4,3,2,1,0:T(8,128)}) fusion(f32[2,512]{1,0:T(2,128)S(1)} %bitcast.173, bf16[1,1,2,512,512]{4,3,2,1,0:T(8,128)(2,1)} %param.7, f32[2,512,512]{1,2,0:T(8,128)S(1)} %fusion.46, bf16[4,2,512,512]{3,2,1,0:T(8,128)(2,1)} %bitcast.158, ...), kind=kOutput, calls=%fused_computation.42 | convolution fusion | flops 2154299392 | bytes 16781320 | tf_op jit(solution)/shard_map/dtij,dtjk->tik/dot_general | solution.py:34
  96.5 4.0 collective-permute-start.7
  102.8 10.4 %collective-permute-done.6 = bf16[1,1,2,512,512]{4,3,2,1,0:T(8,128)(2,1)S(1)} collective-permute-done((bf16[1,1,2,512,512]{4,3,2,1,0:T(8,128)(2,1)S(1)}, bf16[1,1,2,512,512]{4,3,2,1,0:T(8,128)(2,1)S(1)}, u32[]{:S(2)}, u32[]{:S(2)}) %collective-permute-start.6) | collective-permute-done | bytes 1048608 | tf_op jit(solution)/shard_map/ppermute | solution.py:10
  113.1 9.7 %collective-permute-done.8 = bf16[1,1,2,512,512]{4,3,2,1,0:T(8,128)(2,1)S(1)} collective-permute-done((bf16[1,1,2,512,512]{4,3,2,1,0:T(8,128)(2,1)S(1)}, bf16[1,1,2,512,512]{4,3,2,1,0:T(8,128)(2,1)S(1)}, u32[]{:S(2)}, u32[]{:S(2)}) %collective-permute-start.8) | collective-permute-done | bytes 1048608 | tf_op jit(solution)/shard_map/ppermute | solution.py:10
  122.8 2.4 pad_maximum_fusion.2
  125.2 4.9 %gather_fusion.2 = bf16[8,512,512]{2,1,0:T(8,128)(2,1)} fusion(bf16[4,2,512,512]{3,2,1,0:T(8,128)(2,1)} %pad_maximum_fusion.2, s32[8]{0:T(128)S(1)} %reshape.120), kind=kCustom, calls=%fused_computation.2.clone | custom fusion | bytes 8388672 | tf_op jit(solution)/shard_map/vmap(jit(_take))/gather | solution.py:14
  130.2 7.3 %fusion.12 = f32[1,1,2,512,512]{4,3,2,1,0:T(8,128)S(1)} fusion(f32[2,512,512]{1,2,0:T(8,128)S(1)} %fusion.44, f32[1,1,2,512,512]{4,3,2,1,0:T(8,128)} %get-tuple-element.38, f32[1,1,2,512,512]{4,3,2,1,0:T(8,128)} %get-tuple-element.40, bf16[4,2,512,512]{3,2,1,0:T(8,128)(2,1)} %bitcast.156, pred[4,2]{0,1:T(4,128)(4,1)S(1)} %compare_and_fusion, ...), kind=kOutput, calls=%fused_computation.28 | convolution fusion | flops 2153250816 | bytes 16781320 | tf_op jit(solution)/shard_map/dtij,dtjk->tik/dot_general | solution.py:34
  138.8 4.5 %fusion.28 = f32[512,512]{0,1:T(8,128)} fusion(f32[1,1,2,512,512]{4,3,2,1,0:T(8,128)S(1)} %fusion.12), kind=kOutput, calls=%fused_computation.50 | convolution fusion | flops 3221225472 | bytes 3145728 | tf_op jit(solution)/shard_map/ck,cl->kl/dot_general | solution.py:54
  143.4 130.6 %all-reduce.3.cloned.1.call-done = f32[512,512]{0,1:T(8,128)} async-done(((f32[512,512]{0,1:T(8,128)}), f32[512,512]{0,1:T(8,128)}) %all-reduce.3.cloned.1.call-update) | async-done | bytes 1048592 | tf_op jit(solution)/shard_map/psum | solution.py:55
  276.0 11.7 %cholesky.104 = f32[128,128]{1,0:T(8,128)S(1)} custom-call(f32[128,128]{1,0:T(8,128)S(1)} %cholesky.266), custom_call_target="Cholesky" | custom-call | tf_op jit(solution)/shard_map/jit(cholesky)/cholesky | solution.py:57
  287.9 10.0 %custom-call.31 = f32[1,128,128]{1,2,0:T(8,128)S(1)} custom-call(f32[1,128,128]{2,1,0:T(8,128)S(1)} %get-tuple-element.36), custom_call_target="InvertDiagBlocksLowerTriangular" | custom-call | tf_op jit(solution)/shard_map/jit(cholesky)/cholesky | solution.py:57
  298.6 11.7 %cholesky.217 = f32[128,128]{1,0:T(8,128)S(1)} custom-call(f32[128,128]{1,0:T(8,128)S(1)} %cholesky.270), custom_call_target="Cholesky" | custom-call | tf_op jit(solution)/shard_map/jit(cholesky)/cholesky | solution.py:57
  310.3 9.8 %custom-call.32 = f32[1,128,128]{1,2,0:T(8,128)S(1)} custom-call(f32[1,128,128]{2,1,0:T(8,128)S(1)} %get-tuple-element.33), custom_call_target="InvertDiagBlocksLowerTriangular" | custom-call | tf_op jit(solution)/shard_map/jit(cholesky)/cholesky | solution.py:57
  320.8 11.7 %cholesky.238 = f32[128,128]{1,0:T(8,128)S(1)} custom-call(f32[128,128]{1,0:T(8,128)S(1)} %cholesky.275), custom_call_target="Cholesky" | custom-call | tf_op jit(solution)/shard_map/jit(cholesky)/cholesky | solution.py:57
  333.3 10.2 %custom-call.33 = f32[1,128,128]{1,2,0:T(8,128)S(1)} custom-call(f32[1,128,128]{2,1,0:T(8,128)S(1)} %get-tuple-element.30), custom_call_target="InvertDiagBlocksLowerTriangular" | custom-call | tf_op jit(solution)/shard_map/jit(cholesky)/cholesky | solution.py:57
  344.0 11.7 %cholesky.255 = f32[128,128]{1,0:T(8,128)S(1)} custom-call(f32[128,128]{1,0:T(8,128)S(1)} %convolution_subtract_fusion.4), custom_call_target="Cholesky" | custom-call | tf_op jit(solution)/shard_map/jit(cholesky)/cholesky | solution.py:57
  360.8 8.4 %while.1 = (s32[]{:T(128)}, f32[512,512]{1,0:T(8,128)S(1)}, s32[4,2]{0,1:T(2,128)S(1)}, f32[4,128,128]{2,1,0:T(8,128)S(1)}, s32[]{:T(128)}) while((s32[]{:T(128)}, f32[512,512]{1,0:T(8,128)S(1)}, s32[4,2]{0,1:T(2,128)S(1)}, f32[4,128,128]{2,1,0:T(8,128)S(1)}, s32[]{:T(128)}) %tuple.37), condition=%wide.while_cond, body=%wide.while_body.sunk | while | flops 2 | bytes 131181 | solution.py:58
  369.2 39.5 %custom-call.34 = f32[4,128,128]{1,2,0:T(8,128)S(1)} custom-call(f32[4,128,128]{2,1,0:T(8,128)S(1)} %get-tuple-element.10), custom_call_target="InvertDiagBlocksLowerTriangular" | custom-call | tf_op jit(solution)/shard_map/jit(_solve_triangular)/triangular_solve | solution.py:58
  413.0 2.9 convolution_subtract_fusion
  416.5 3.8 fusion.37
  422.9 2.5 copy.34
  (77 shorter events, 36.1 us)
Async XLA Ops:
  7.2 9.4 %copy-start = (bf16[1,1,2,512,512]{4,3,2,1,0:T(8,128)(2,1)S(1)}, bf16[1,1,2,512,512]{4,3,2,1,0:T(8,128)(2,1)}, u32[]{:S(2)}) copy-start(bf16[1,1,2,512,512]{4,3,2,1,0:T(8,128)(2,1)} %param.8) | copy-start | bytes 3145732
  7.2 9.3 %copy-start.5 = (f32[1,1,2,512]{3,2,1,0:T(2,128)S(1)}, f32[1,1,2,512]{3,2,1,0:T(2,128)}, u32[]{:S(2)}) copy-start(f32[1,1,2,512]{3,2,1,0:T(2,128)} %param.11) | copy-start | bytes 12292
  7.2 9.1 %copy-start.6 = (s32[1,1,4,2]{2,3,1,0:T(2,128)S(1)}, s32[1,1,4,2]{2,3,1,0:T(2,128)}, u32[]{:S(2)}) copy-start(s32[1,1,4,2]{2,3,1,0:T(2,128)} %param.10) | copy-start | bytes 100
  7.2 266.8 %all-reduce.3.cloned.1.call-start = ((), (), s32[]{:S(2)}) async-start(), calls=%async_computation | async-start | bytes 2097152 | tf_op jit(solution)/shard_map/psum | solution.py:55
  8.8 18.1 %collective-permute-start = (bf16[1,1,2,512,512]{4,3,2,1,0:T(8,128)(2,1)S(1)}, bf16[1,1,2,512,512]{4,3,2,1,0:T(8,128)(2,1)S(1)}, u32[]{:S(2)}, u32[]{:S(2)}) collective-permute-start(bf16[1,1,2,512,512]{4,3,2,1,0:T(8,128)(2,1)S(1)} %fusion.10), channel_id=1, source_target_pairs={{30,0},{0,2},{2,4},{4,6},{6,8},{8,10},{10,12},{12,14},{14,16},{16,... | collective-permute-start | bytes 3145736 | tf_op jit(solution)/shard_map/ppermute | solution.py:10
  9.4 17.6 %collective-permute-start.1 = (bf16[1,1,2,512,512]{4,3,2,1,0:T(8,128)(2,1)S(1)}, bf16[1,1,2,512,512]{4,3,2,1,0:T(8,128)(2,1)}, u32[]{:S(2)}, u32[]{:S(2)}) collective-permute-start(bf16[1,1,2,512,512]{4,3,2,1,0:T(8,128)(2,1)S(1)} %fusion.10), channel_id=1, source_target_pairs={{2,0},{4,2},{6,4},{8,6},{10,8},{12,10},{14,12},{16,14},{18,16},{20... | collective-permute-start | bytes 3145736 | tf_op jit(solution)/shard_map/ppermute | solution.py:10
  14.4 22.7 %collective-permute-start.2 = (bf16[1,1,2,512,512]{4,3,2,1,0:T(8,128)(2,1)S(1)}, bf16[1,1,2,512,512]{4,3,2,1,0:T(8,128)(2,1)}, u32[]{:S(2)}, u32[]{:S(2)}) collective-permute-start(bf16[1,1,2,512,512]{4,3,2,1,0:T(8,128)(2,1)S(1)} %fusion.10), channel_id=1, source_target_pairs={{1,0},{0,1},{3,2},{2,3},{5,4},{4,5},{7,6},{6,7},{9,8},{8,9},{11,10... | collective-permute-start | bytes 3145736 | tf_op jit(solution)/shard_map/ppermute | solution.py:10
  41.1 5.1 %copy-start.4 = (f32[2,512,512]{1,2,0:T(8,128)S(1)}, f32[2,512,512]{1,2,0:T(8,128)}, u32[]{:S(2)}) copy-start(f32[2,512,512]{1,2,0:T(8,128)} %fusion.48) | copy-start | bytes 6291460
  53.8 17.0 %collective-permute-start.3 = (bf16[1,1,2,512,512]{4,3,2,1,0:T(8,128)(2,1)S(1)}, bf16[1,1,2,512,512]{4,3,2,1,0:T(8,128)(2,1)S(1)}, u32[]{:S(2)}, u32[]{:S(2)}) collective-permute-start(bf16[1,1,2,512,512]{4,3,2,1,0:T(8,128)(2,1)S(1)} %get-tuple-element.37), channel_id=1, source_target_pairs={{30,0},{0,2},{2,4},{4,6},{6,8},{8,10},{10,12},{12,14},{14,16},{16,... | collective-permute-start | bytes 3145736 | tf_op jit(solution)/shard_map/ppermute | solution.py:10
  54.2 16.6 %collective-permute-start.4 = (bf16[1,1,2,512,512]{4,3,2,1,0:T(8,128)(2,1)S(1)}, bf16[1,1,2,512,512]{4,3,2,1,0:T(8,128)(2,1)S(1)}, u32[]{:S(2)}, u32[]{:S(2)}) collective-permute-start(bf16[1,1,2,512,512]{4,3,2,1,0:T(8,128)(2,1)S(1)} %get-tuple-element.37), channel_id=1, source_target_pairs={{2,0},{4,2},{6,4},{8,6},{10,8},{12,10},{14,12},{16,14},{18,16},{20... | collective-permute-start | bytes 3145736 | tf_op jit(solution)/shard_map/ppermute | solution.py:10
  58.2 22.3 %collective-permute-start.5 = (bf16[1,1,2,512,512]{4,3,2,1,0:T(8,128)(2,1)S(1)}, bf16[1,1,2,512,512]{4,3,2,1,0:T(8,128)(2,1)S(1)}, u32[]{:S(2)}, u32[]{:S(2)}) collective-permute-start(bf16[1,1,2,512,512]{4,3,2,1,0:T(8,128)(2,1)S(1)} %get-tuple-element.37), channel_id=1, source_target_pairs={{1,0},{0,1},{3,2},{2,3},{5,4},{4,5},{7,6},{6,7},{9,8},{8,9},{11,10... | collective-permute-start | bytes 3145736 | tf_op jit(solution)/shard_map/ppermute | solution.py:10
  96.1 17.0 %collective-permute-start.6 = (bf16[1,1,2,512,512]{4,3,2,1,0:T(8,128)(2,1)S(1)}, bf16[1,1,2,512,512]{4,3,2,1,0:T(8,128)(2,1)S(1)}, u32[]{:S(2)}, u32[]{:S(2)}) collective-permute-start(bf16[1,1,2,512,512]{4,3,2,1,0:T(8,128)(2,1)S(1)} %get-tuple-element.39), channel_id=1, source_target_pairs={{30,0},{0,2},{2,4},{4,6},{6,8},{8,10},{10,12},{12,14},{14,16},{16,... | collective-permute-start | bytes 3145736 | tf_op jit(solution)/shard_map/ppermute | solution.py:10
  96.5 16.6 %collective-permute-start.7 = (bf16[1,1,2,512,512]{4,3,2,1,0:T(8,128)(2,1)S(1)}, bf16[1,1,2,512,512]{4,3,2,1,0:T(8,128)(2,1)S(1)}, u32[]{:S(2)}, u32[]{:S(2)}) collective-permute-start(bf16[1,1,2,512,512]{4,3,2,1,0:T(8,128)(2,1)S(1)} %get-tuple-element.39), channel_id=1, source_target_pairs={{2,0},{4,2},{6,4},{8,6},{10,8},{12,10},{14,12},{16,14},{18,16},{20... | collective-permute-start | bytes 3145736 | tf_op jit(solution)/shard_map/ppermute | solution.py:10
  100.6 22.3 %collective-permute-start.8 = (bf16[1,1,2,512,512]{4,3,2,1,0:T(8,128)(2,1)S(1)}, bf16[1,1,2,512,512]{4,3,2,1,0:T(8,128)(2,1)S(1)}, u32[]{:S(2)}, u32[]{:S(2)}) collective-permute-start(bf16[1,1,2,512,512]{4,3,2,1,0:T(8,128)(2,1)S(1)} %get-tuple-element.39), channel_id=1, source_target_pairs={{1,0},{0,1},{3,2},{2,3},{5,4},{4,5},{7,6},{6,7},{9,8},{8,9},{11,10... | collective-permute-start | bytes 3145736 | tf_op jit(solution)/shard_map/ppermute | solution.py:10
  137.5 1.3 copy-start.3
  274.0 1.8 copy-start.2
  421.1 4.4 %copy-start.1 = (bf16[1,1,2,512,512]{4,3,2,1,0:T(8,128)(2,1)S(1)}, bf16[1,1,2,512,512]{4,3,2,1,0:T(8,128)(2,1)}, u32[]{:S(2)}) copy-start(bf16[1,1,2,512,512]{4,3,2,1,0:T(8,128)(2,1)} %param.8) | copy-start | bytes 3145732
Sparse Core Ops, SparseCore 0:
  143.5 130.4 all-reduce.2
where the time goes:
time: 439 us; the launch traced here: 432 us
  waiting for transfers between devices  189 us (43%)
  other arithmetic  132 us (30%)
  matrix products  45.4 us (10%)
  local copies, waits for them, and re-layouts  29.7 us (7%)
  starting transfers between devices  19.4 us (4%)
  between operations  17 us (4%)
    psum x1, waiting for transfers between devices, body(): gram = lax.psum(local_gram, ('gy', 'gz'))  131 us
    another operation x14, other arithmetic, body(): lower = jnp.linalg.cholesky(gram)  78.9 us
    ppermute x9, waiting for transfers between devices, shifted(): return lax.ppermute(block, axis, route)  58.7 us
    another operation x2, other arithmetic, body(): basis = jax.scipy.linalg.solve_triangular(lower, flat.T, lower=True).T  39.5 us
    dot_general x3, matrix products, apply_scaled(): jnp.einsum('dtij,dtjk->tik', couple_ops[0, 0], picked, preferred_element_...  23.3 us
    ppermute x9, starting transfers between devices, shifted(): return lax.ppermute(block, axis, route)  19.3 us
    gather x5, local copies, waits for them, and re-layouts, pick_tiles(): return jnp.take(blocks, indices, axis=0)  15.2 us
    another operation x7, matrix products, body(): basis = jax.scipy.linalg.solve_triangular(lower, flat.T, lower=True).T  12.3 us
  transfers between devices with their start and end apart: 10, of which 7 were waited for; matrix products, arithmetic and copies ran while one was open for 1% of the time, Pallas kernels for 0%

commit v1 on v0

--- a/solution.py
+++ b/solution.py
@@ -52,7 +52,11 @@
     flat = fourth.reshape(-1, width)
     total_cells = flat.shape[0] * lax.axis_size("gy") * lax.axis_size("gz")
     local_gram = jnp.einsum("ck,cl->kl", flat, flat, precision=lax.Precision.HIGHEST)
-    gram = lax.psum(local_gram, ("gy", "gz"))
+
+    def perform_patches(arr_in):
+        return jnp.sum(lax.all_gather(arr_in, axis_name=("gy", "gz")), axis=0)
+
+    gram = perform_patches(local_gram)
     gram = gram / jnp.float32(total_cells)
     lower = jnp.linalg.cholesky(gram)
     basis = jax.scipy.linalg.solve_triangular(lower, flat.T, lower=True).T

time: 439 us -> 523 us (1.19)
  waiting for transfers between devices: 189 us -> 251 us
  other arithmetic: 132 us -> 145 us
  local copies, waits for them, and re-layouts: 29.7 us -> 38.9 us
    all_gather x0 -> x1, waiting for transfers between devices: none -> 192 us  [perform_patches(): return jnp.sum(lax.all_gather(arr_in, axis_name=('gy', 'gz')), axis=0)]
    psum x1 -> x0, waiting for transfers between devices: 131 us -> none  [body(): gram = lax.psum(local_gram, ('gy', 'gz'))]
    reduce_sum x0 -> x1, other arithmetic: none -> 12.4 us  [perform_patches(): return jnp.sum(lax.all_gather(arr_in, axis_name=('gy', 'gz')), axis=0)]
    another operation x12, local copies, waits for them, and re-layouts: 8.31 us -> 13.7 us
  transfers between devices with their start and end apart: 10 -> 10, of which waited for: 7 -> 8; matrix products, arithmetic and copies ran while one was open for 1% -> 1% of each run, Pallas kernels for 0% -> 0%
where the time goes in v1:
time: 523 us; the launch traced here: 516 us
  waiting for transfers between devices  251 us (48%)
  other arithmetic  145 us (28%)
  matrix products  44.3 us (8%)
  local copies, waits for them, and re-layouts  38.9 us (7%)
  starting transfers between devices  19.9 us (4%)
  between operations  17.3 us (3%)
    all_gather x1, waiting for transfers between devices, perform_patches(): return jnp.sum(lax.all_gather(arr_in, axis_name=('gy', 'gz')), axis=0)  192 us
    another operation x14, other arithmetic, body(): lower = jnp.linalg.cholesky(gram)  78.6 us
    ppermute x9, waiting for transfers between devices, shifted(): return lax.ppermute(block, axis, route)  58.8 us
    another operation x2, other arithmetic, body(): basis = jax.scipy.linalg.solve_triangular(lower, flat.T, lower=True).T  40.1 us
    dot_general x3, matrix products, apply_scaled(): jnp.einsum('dtij,dtjk->tik', couple_ops[0, 0], picked, preferred_element_...  23.3 us
    ppermute x9, starting transfers between devices, shifted(): return lax.ppermute(block, axis, route)  19.8 us
    gather x5, local copies, waits for them, and re-layouts, pick_tiles(): return jnp.take(blocks, indices, axis=0)  15.2 us
    another operation x12, local copies, waits for them, and re-layouts  13.7 us
  transfers between devices with their start and end apart: 10, of which 8 were waited for; matrix products, arithmetic and copies ran while one was open for 1% of the time, Pallas kernels for 0%

profile of v1, /device:TPU:0, one launch (start us, length us, event | category | flops | bytes accessed | tf_op | source)
XLA Modules:
  0.0 516.0 jit_solution(2633133458906682429)
XLA Ops:
  9.4 5.0 collective-permute-start.1
  18.6 8.4 %collective-permute-done = bf16[1,1,2,512,512]{4,3,2,1,0:T(8,128)(2,1)S(1)} collective-permute-done((bf16[1,1,2,512,512]{4,3,2,1,0:T(8,128)(2,1)S(1)}, bf16[1,1,2,512,512]{4,3,2,1,0:T(8,128)(2,1)S(1)}, u32[]{:S(2)}, u32[]{:S(2)}) %collective-permute-start) | collective-permute-done | bytes 1048608 | tf_op jit(solution)/shard_map/ppermute | solution.py:10
  27.0 10.2 %collective-permute-done.2 = bf16[1,1,2,512,512]{4,3,2,1,0:T(8,128)(2,1)} collective-permute-done((bf16[1,1,2,512,512]{4,3,2,1,0:T(8,128)(2,1)S(1)}, bf16[1,1,2,512,512]{4,3,2,1,0:T(8,128)(2,1)}, u32[]{:S(2)}, u32[]{:S(2)}) %collective-permute-start.2) | collective-permute-done | bytes 1048608 | tf_op jit(solution)/shard_map/ppermute | solution.py:10
  37.2 3.9 pad_maximum_fusion
  41.1 5.1 gather_fusion
  46.2 7.5 %multiply_convert_fusion.1 = (bf16[1,1,2,512,512]{4,3,2,1,0:T(8,128)(2,1)S(1)}, f32[1,1,2,512,512]{4,3,2,1,0:T(8,128)}) fusion(f32[2,512]{1,0:T(2,128)S(1)} %broadcast_multiply_fusion, f32[2,512,512]{1,2,0:T(8,128)S(1)} %copy-done.3, bf16[4,2,512,512]{3,2,1,0:T(8,128)(2,1)} %bitcast.162, pred[4,2]{0,1:T(4,128)(4,1)S(1)} %compare_and_fusion, ...), kind=kOutput, calls=%fused_computation.43 | convolution fusion | flops 2153250816 | bytes 14688264 | tf_op jit(solution)/shard_map/dtij,dtjk->tik/dot_general | solution.py:34
  54.2 4.0 collective-permute-start.4
  60.4 10.4 %collective-permute-done.3 = bf16[1,1,2,512,512]{4,3,2,1,0:T(8,128)(2,1)S(1)} collective-permute-done((bf16[1,1,2,512,512]{4,3,2,1,0:T(8,128)(2,1)S(1)}, bf16[1,1,2,512,512]{4,3,2,1,0:T(8,128)(2,1)S(1)}, u32[]{:S(2)}, u32[]{:S(2)}) %collective-permute-start.3) | collective-permute-done | bytes 1048608 | tf_op jit(solution)/shard_map/ppermute | solution.py:10
  70.8 9.7 %collective-permute-done.5 = bf16[1,1,2,512,512]{4,3,2,1,0:T(8,128)(2,1)S(1)} collective-permute-done((bf16[1,1,2,512,512]{4,3,2,1,0:T(8,128)(2,1)S(1)}, bf16[1,1,2,512,512]{4,3,2,1,0:T(8,128)(2,1)S(1)}, u32[]{:S(2)}, u32[]{:S(2)}) %collective-permute-start.5) | collective-permute-done | bytes 1048608 | tf_op jit(solution)/shard_map/ppermute | solution.py:10
  82.7 4.9 gather_fusion.1
  87.7 8.4 %multiply_convert_fusion = (bf16[1,1,2,512,512]{4,3,2,1,0:T(8,128)(2,1)S(1)}, f32[1,1,2,512,512]{4,3,2,1,0:T(8,128)}) fusion(f32[2,512]{1,0:T(2,128)S(1)} %bitcast.175, bf16[1,1,2,512,512]{4,3,2,1,0:T(8,128)(2,1)} %param.7, f32[2,512,512]{1,2,0:T(8,128)S(1)} %fusion.46, bf16[4,2,512,512]{3,2,1,0:T(8,128)(2,1)} %bitcast.163, ...), kind=kOutput, calls=%fused_computation.42 | convolution fusion | flops 2154299392 | bytes 16781320 | tf_op jit(solution)/shard_map/dtij,dtjk->tik/dot_general | solution.py:34
  96.5 4.5 collective-permute-start.7
  103.3 9.9 %collective-permute-done.6 = bf16[1,1,2,512,512]{4,3,2,1,0:T(8,128)(2,1)S(1)} collective-permute-done((bf16[1,1,2,512,512]{4,3,2,1,0:T(8,128)(2,1)S(1)}, bf16[1,1,2,512,512]{4,3,2,1,0:T(8,128)(2,1)S(1)}, u32[]{:S(2)}, u32[]{:S(2)}) %collective-permute-start.6) | collective-permute-done | bytes 1048608 | tf_op jit(solution)/shard_map/ppermute | solution.py:10
  113.4 10.0 %collective-permute-done.8 = bf16[1,1,2,512,512]{4,3,2,1,0:T(8,128)(2,1)S(1)} collective-permute-done((bf16[1,1,2,512,512]{4,3,2,1,0:T(8,128)(2,1)S(1)}, bf16[1,1,2,512,512]{4,3,2,1,0:T(8,128)(2,1)S(1)}, u32[]{:S(2)}, u32[]{:S(2)}) %collective-permute-start.8) | collective-permute-done | bytes 1048608 | tf_op jit(solution)/shard_map/ppermute | solution.py:10
  125.7 4.9 gather_fusion.2
  130.6 7.3 %fusion.12 = f32[1,1,2,512,512]{4,3,2,1,0:T(8,128)S(1)} fusion(f32[2,512,512]{1,2,0:T(8,128)S(1)} %fusion.44, f32[1,1,2,512,512]{4,3,2,1,0:T(8,128)} %get-tuple-element.40, f32[1,1,2,512,512]{4,3,2,1,0:T(8,128)} %get-tuple-element.42, bf16[4,2,512,512]{3,2,1,0:T(8,128)(2,1)} %bitcast.161, pred[4,2]{0,1:T(4,128)(4,1)S(1)} %compare_and_fusion, ...), kind=kOutput, calls=%fused_computation.28 | convolution fusion | flops 2153250816 | bytes 16781320 | tf_op jit(solution)/shard_map/dtij,dtjk->tik/dot_general | solution.py:34
  139.2 4.5 fusion.28
  145.7 192.3 %all-gather.3.cloned.1.call-done = f32[16384,512]{1,0:T(8,128)} async-done(((f32[512,512]{1,0:T(8,128)}), f32[16384,512]{1,0:T(8,128)}) %all-gather.3.cloned.1.call-update) | async-done | bytes 33554448 | tf_op jit(solution)/shard_map/all_gather | solution.py:57
  338.0 12.4 %reduce_sum.11 = f32[512,512]{1,0:T(8,128)S(1)} reduce(f32[32,512,512]{2,1,0:T(8,128)} %bitcast.156, f32[]{:T(128)} %constant.165.clone.1), dimensions={0}, to_apply=%region_0.0 | reduce | flops 8126464 | bytes 34603012 | tf_op jit(solution)/shard_map/reduce_sum | solution.py:57
  354.2 11.7 %cholesky.104 = f32[128,128]{1,0:T(8,128)S(1)} custom-call(f32[128,128]{1,0:T(8,128)S(1)} %cholesky.266), custom_call_target="Cholesky" | custom-call | tf_op jit(solution)/shard_map/jit(cholesky)/cholesky | solution.py:61
  366.1 9.8 %custom-call.31 = f32[1,128,128]{1,2,0:T(8,128)S(1)} custom-call(f32[1,128,128]{2,1,0:T(8,128)S(1)} %get-tuple-element.38), custom_call_target="InvertDiagBlocksLowerTriangular" | custom-call | tf_op jit(solution)/shard_map/jit(cholesky)/cholesky | solution.py:61
  378.4 11.7 %cholesky.217 = f32[128,128]{1,0:T(8,128)S(1)} custom-call(f32[128,128]{1,0:T(8,128)S(1)} %cholesky.270), custom_call_target="Cholesky" | custom-call | tf_op jit(solution)/shard_map/jit(cholesky)/cholesky | solution.py:61
  390.2 10.0 %custom-call.32 = f32[1,128,128]{1,2,0:T(8,128)S(1)} custom-call(f32[1,128,128]{2,1,0:T(8,128)S(1)} %get-tuple-element.35), custom_call_target="InvertDiagBlocksLowerTriangular" | custom-call | tf_op jit(solution)/shard_map/jit(cholesky)/cholesky | solution.py:61
  401.7 11.7 %cholesky.238 = f32[128,128]{1,0:T(8,128)S(1)} custom-call(f32[128,128]{1,0:T(8,128)S(1)} %cholesky.275), custom_call_target="Cholesky" | custom-call | tf_op jit(solution)/shard_map/jit(cholesky)/cholesky | solution.py:61
  414.2 9.8 %custom-call.33 = f32[1,128,128]{1,2,0:T(8,128)S(1)} custom-call(f32[1,128,128]{2,1,0:T(8,128)S(1)} %get-tuple-element.32), custom_call_target="InvertDiagBlocksLowerTriangular" | custom-call | tf_op jit(solution)/shard_map/jit(cholesky)/cholesky | solution.py:61
  425.4 11.7 %cholesky.255 = f32[128,128]{1,0:T(8,128)S(1)} custom-call(f32[128,128]{1,0:T(8,128)S(1)} %convolution_subtract_fusion.4), custom_call_target="Cholesky" | custom-call | tf_op jit(solution)/shard_map/jit(cholesky)/cholesky | solution.py:61
  442.8 13.7 %while.1 = (s32[]{:T(128)}, f32[512,512]{1,0:T(8,128)}, s32[4,2]{0,1:T(2,128)S(1)}, f32[4,128,128]{2,1,0:T(8,128)}, s32[]{:T(128)}) while((s32[]{:T(128)}, f32[512,512]{1,0:T(8,128)}, s32[4,2]{0,1:T(2,128)S(1)}, f32[4,128,128]{2,1,0:T(8,128)}, s32[]{:T(128)}) %tuple.38), condition=%wide.while_cond, body=%wide.while_body.sunk | while | flops 2 | bytes 132705 | solution.py:62
  443.4 2.8 bitcast_dynamic-update-slice_fusion.2
  446.8 2.8 bitcast_dynamic-update-slice_fusion.2
  450.2 2.8 bitcast_dynamic-update-slice_fusion.2
  453.7 2.8 bitcast_dynamic-update-slice_fusion.2
  456.4 40.1 %custom-call.34 = f32[4,128,128]{1,2,0:T(8,128)S(1)} custom-call(f32[4,128,128]{2,1,0:T(8,128)} %get-tuple-element.10), custom_call_target="InvertDiagBlocksLowerTriangular" | custom-call | tf_op jit(solution)/shard_map/jit(_solve_triangular)/triangular_solve | solution.py:62
  (78 shorter events, 47.2 us)
Async XLA Ops:
  7.2 9.4 %copy-start = (bf16[1,1,2,512,512]{4,3,2,1,0:T(8,128)(2,1)S(1)}, bf16[1,1,2,512,512]{4,3,2,1,0:T(8,128)(2,1)}, u32[]{:S(2)}) copy-start(bf16[1,1,2,512,512]{4,3,2,1,0:T(8,128)(2,1)} %param.8) | copy-start | bytes 3145732
  7.2 9.3 %copy-start.5 = (f32[1,1,2,512]{3,2,1,0:T(2,128)S(1)}, f32[1,1,2,512]{3,2,1,0:T(2,128)}, u32[]{:S(2)}) copy-start(f32[1,1,2,512]{3,2,1,0:T(2,128)} %param.11) | copy-start | bytes 12292
  7.2 9.1 %copy-start.6 = (s32[1,1,4,2]{2,3,1,0:T(2,128)S(1)}, s32[1,1,4,2]{2,3,1,0:T(2,128)}, u32[]{:S(2)}) copy-start(s32[1,1,4,2]{2,3,1,0:T(2,128)} %param.10) | copy-start | bytes 100
  7.2 330.8 %all-gather.3.cloned.1.call-start = ((), (), s32[]{:S(2)}) async-start(), calls=%async_computation | async-start | bytes 34603008 | tf_op jit(solution)/shard_map/all_gather | solution.py:57
  8.8 18.1 %collective-permute-start = (bf16[1,1,2,512,512]{4,3,2,1,0:T(8,128)(2,1)S(1)}, bf16[1,1,2,512,512]{4,3,2,1,0:T(8,128)(2,1)S(1)}, u32[]{:S(2)}, u32[]{:S(2)}) collective-permute-start(bf16[1,1,2,512,512]{4,3,2,1,0:T(8,128)(2,1)S(1)} %fusion.10), channel_id=1, source_target_pairs={{30,0},{0,2},{2,4},{4,6},{6,8},{8,10},{10,12},{12,14},{14,16},{16,... | collective-permute-start | bytes 3145736 | tf_op jit(solution)/shard_map/ppermute | solution.py:10
  9.4 17.6 %collective-permute-start.1 = (bf16[1,1,2,512,512]{4,3,2,1,0:T(8,128)(2,1)S(1)}, bf16[1,1,2,512,512]{4,3,2,1,0:T(8,128)(2,1)}, u32[]{:S(2)}, u32[]{:S(2)}) collective-permute-start(bf16[1,1,2,512,512]{4,3,2,1,0:T(8,128)(2,1)S(1)} %fusion.10), channel_id=1, source_target_pairs={{2,0},{4,2},{6,4},{8,6},{10,8},{12,10},{14,12},{16,14},{18,16},{20... | collective-permute-start | bytes 3145736 | tf_op jit(solution)/shard_map/ppermute | solution.py:10
  14.4 22.7 %collective-permute-start.2 = (bf16[1,1,2,512,512]{4,3,2,1,0:T(8,128)(2,1)S(1)}, bf16[1,1,2,512,512]{4,3,2,1,0:T(8,128)(2,1)}, u32[]{:S(2)}, u32[]{:S(2)}) collective-permute-start(bf16[1,1,2,512,512]{4,3,2,1,0:T(8,128)(2,1)S(1)} %fusion.10), channel_id=1, source_target_pairs={{1,0},{0,1},{3,2},{2,3},{5,4},{4,5},{7,6},{6,7},{9,8},{8,9},{11,10... | collective-permute-start | bytes 3145736 | tf_op jit(solution)/shard_map/ppermute | solution.py:10
  41.1 5.1 copy-start.3
  53.8 17.0 %collective-permute-start.3 = (bf16[1,1,2,512,512]{4,3,2,1,0:T(8,128)(2,1)S(1)}, bf16[1,1,2,512,512]{4,3,2,1,0:T(8,128)(2,1)S(1)}, u32[]{:S(2)}, u32[]{:S(2)}) collective-permute-start(bf16[1,1,2,512,512]{4,3,2,1,0:T(8,128)(2,1)S(1)} %get-tuple-element.39), channel_id=1, source_target_pairs={{30,0},{0,2},{2,4},{4,6},{6,8},{8,10},{10,12},{12,14},{14,16},{16,... | collective-permute-start | bytes 3145736 | tf_op jit(solution)/shard_map/ppermute | solution.py:10
  54.2 16.6 %collective-permute-start.4 = (bf16[1,1,2,512,512]{4,3,2,1,0:T(8,128)(2,1)S(1)}, bf16[1,1,2,512,512]{4,3,2,1,0:T(8,128)(2,1)S(1)}, u32[]{:S(2)}, u32[]{:S(2)}) collective-permute-start(bf16[1,1,2,512,512]{4,3,2,1,0:T(8,128)(2,1)S(1)} %get-tuple-element.39), channel_id=1, source_target_pairs={{2,0},{4,2},{6,4},{8,6},{10,8},{12,10},{14,12},{16,14},{18,16},{20... | collective-permute-start | bytes 3145736 | tf_op jit(solution)/shard_map/ppermute | solution.py:10
  58.2 22.3 %collective-permute-start.5 = (bf16[1,1,2,512,512]{4,3,2,1,0:T(8,128)(2,1)S(1)}, bf16[1,1,2,512,512]{4,3,2,1,0:T(8,128)(2,1)S(1)}, u32[]{:S(2)}, u32[]{:S(2)}) collective-permute-start(bf16[1,1,2,512,512]{4,3,2,1,0:T(8,128)(2,1)S(1)} %get-tuple-element.39), channel_id=1, source_target_pairs={{1,0},{0,1},{3,2},{2,3},{5,4},{4,5},{7,6},{6,7},{9,8},{8,9},{11,10... | collective-permute-start | bytes 3145736 | tf_op jit(solution)/shard_map/ppermute | solution.py:10
  96.1 17.0 %collective-permute-start.6 = (bf16[1,1,2,512,512]{4,3,2,1,0:T(8,128)(2,1)S(1)}, bf16[1,1,2,512,512]{4,3,2,1,0:T(8,128)(2,1)S(1)}, u32[]{:S(2)}, u32[]{:S(2)}) collective-permute-start(bf16[1,1,2,512,512]{4,3,2,1,0:T(8,128)(2,1)S(1)} %get-tuple-element.41), channel_id=1, source_target_pairs={{30,0},{0,2},{2,4},{4,6},{6,8},{8,10},{10,12},{12,14},{14,16},{16,... | collective-permute-start | bytes 3145736 | tf_op jit(solution)/shard_map/ppermute | solution.py:10
  96.5 16.9 %collective-permute-start.7 = (bf16[1,1,2,512,512]{4,3,2,1,0:T(8,128)(2,1)S(1)}, bf16[1,1,2,512,512]{4,3,2,1,0:T(8,128)(2,1)S(1)}, u32[]{:S(2)}, u32[]{:S(2)}) collective-permute-start(bf16[1,1,2,512,512]{4,3,2,1,0:T(8,128)(2,1)S(1)} %get-tuple-element.41), channel_id=1, source_target_pairs={{2,0},{4,2},{6,4},{8,6},{10,8},{12,10},{14,12},{16,14},{18,16},{20... | collective-permute-start | bytes 3145736 | tf_op jit(solution)/shard_map/ppermute | solution.py:10
  101.1 22.3 %collective-permute-start.8 = (bf16[1,1,2,512,512]{4,3,2,1,0:T(8,128)(2,1)S(1)}, bf16[1,1,2,512,512]{4,3,2,1,0:T(8,128)(2,1)S(1)}, u32[]{:S(2)}, u32[]{:S(2)}) collective-permute-start(bf16[1,1,2,512,512]{4,3,2,1,0:T(8,128)(2,1)S(1)} %get-tuple-element.41), channel_id=1, source_target_pairs={{1,0},{0,1},{3,2},{2,3},{5,4},{4,5},{7,6},{6,7},{9,8},{8,9},{11,10... | collective-permute-start | bytes 3145736 | tf_op jit(solution)/shard_map/ppermute | solution.py:10
  137.9 1.3 copy-start.4
  353.2 1.0 copy-start.2
  504.4 4.4 copy-start.1
Sparse Core Ops, SparseCore 0:
  143.9 194.0 all-gather.2
